TPU v7x, 256 devices: a whole 4x4x8 slice. The times are simulated.
256 devices in a mesh: tm: 16 (over z, core), panel: 16 (over y, x).
Axes of the slice: x: 4, y: 4, z: 8, core: 2. Of those that a mesh axis runs over, the one named last changes fastest.
Arguments:
- dynamics: bfloat16 [16, 1536, 1536], P('tm', 'panel'), may hold values from -1 to 1
- coupling: bfloat16 [16, 1536, 1536], P('tm', 'panel'), may hold values from -1 to 1
- cost_matrix: bfloat16 [16, 1536, 1536], P('tm', 'panel'), may hold values from -1 to 1
- band_offset: int32 [16, 12], P('tm'), may hold values from -1 to 0
- band_width: int32 [16, 12], P('tm'), may hold values from 2 to 3
Outputs:
- level_one: bfloat16 [16, 3, 1536, 1536], P('tm', None, 'panel')
- level_two: bfloat16 [16, 3, 1536, 1536], P('tm', None, 'panel')
All inputs are finite; a program needn't handle non-finite values.
Results may differ from a plain program's by a relative error of at most 0.012.
The roundings to bfloat16 on the way count: a program that leaves them out, or rounds other values in their place, can miss the bound.
Values may be sent and summed in bfloat16 or wider, within the bound.
A program may use at most 128 MiB of HBM per device.

v0:
```python
import jax
import jax.numpy as jnp
from jax import lax
from jax.sharding import PartitionSpec as P

BLOCK = 128
LEVELS = 2


def passed_along(value, axis, by):
    count = lax.axis_size(axis)
    pairs = [(i, i + by) for i in range(count) if 0 <= i + by < count]
    return lax.ppermute(value, axis, pairs)


def contract_rows(left, piece):
    return jnp.dot(left, piece, preferred_element_type=jnp.float32)


def contract_columns(whole, first, count, piece):
    block = lax.dynamic_slice(whole, (0, first), (piece.shape[0], count))
    return lax.dot_general(
        block, piece, (((0,), (0,)), ((), ())), preferred_element_type=jnp.float32
    )


def level_step(element, distance, first):
    a_own, c_own, j_own = element
    rows, width = a_own.shape
    a_part, c_part, j_prev = passed_along((a_own, c_own, j_own), "tm", distance)
    a_prev, c_prev = (
        lax.all_gather(a_part, "panel", axis=0, tiled=True),
        lax.all_gather(c_part, "panel", axis=0, tiled=True),
    )
    a_full, j_full = (
        lax.all_gather(a_own, "panel", axis=0, tiled=True),
        lax.all_gather(j_own, "panel", axis=0, tiled=True),
    )
    k_rows = jnp.dot(c_part, j_full, preferred_element_type=jnp.float32).astype(jnp.bfloat16)
    q_rows = contract_rows(k_rows, lax.all_gather(k_rows, "panel", axis=0, tiled=True)).astype(
        jnp.bfloat16
    )
    k_q = contract_rows(k_rows, lax.all_gather(q_rows, "panel", axis=0, tiled=True))
    row_ids = first + jnp.arange(rows, dtype=jnp.int32)
    identity = (row_ids[:, None] == jnp.arange(width, dtype=jnp.int32)[None, :]).astype(jnp.float32)
    x_rows = (identity - k_rows.astype(jnp.float32) + q_rows.astype(jnp.float32) - k_q).astype(
        jnp.bfloat16
    )
    u_rows = jnp.dot(x_rows, a_prev, preferred_element_type=jnp.float32).astype(jnp.bfloat16)
    a_sum = contract_rows(a_own, lax.all_gather(u_rows, "panel", axis=0, tiled=True))
    s_sum = contract_rows(j_own, lax.all_gather(u_rows, "panel", axis=0, tiled=True))
    a_new = a_sum.astype(jnp.bfloat16)
    s_rows = s_sum.astype(jnp.bfloat16)
    v_rows = jnp.dot(x_rows, c_prev, preferred_element_type=jnp.float32).astype(jnp.bfloat16)
    w_rows = contract_rows(a_own, lax.all_gather(v_rows, "panel", axis=0, tiled=True)).astype(
        jnp.bfloat16
    )
    c_sum = lax.dot_general(
        w_rows, a_full, (((1,), (1,)), ((), ())), preferred_element_type=jnp.float32
    )
    c_new = (c_sum + c_own.astype(jnp.float32)).astype(jnp.bfloat16)
    j_sum = contract_columns(
        a_prev, first, rows, lax.all_gather(s_rows, "panel", axis=0, tiled=True)
    )
    j_new = (j_sum + j_prev.astype(jnp.float32)).astype(jnp.bfloat16)
    valid = lax.axis_index("tm") >= distance
    return (
        jnp.where(valid, a_new, a_own),
        jnp.where(valid, c_new, c_own),
        jnp.where(valid, j_new, j_own),
    )


def shards(dynamics, coupling, cost_matrix, band_offset, band_width):
    rows = dynamics.shape[1]
    width = dynamics.shape[2]
    first = lax.axis_index("panel") * rows
    row_block = (first + jnp.arange(rows, dtype=jnp.int32)) // BLOCK
    block_ids = jnp.arange(width // BLOCK, dtype=jnp.int32)
    picked = row_block[:, None] == block_ids[None, :]
    offsets = jnp.sum(jnp.where(picked, band_offset[0][None, :], 0), axis=1)
    widths = jnp.sum(jnp.where(picked, band_width[0][None, :], 0), axis=1)
    col_block = jnp.arange(width, dtype=jnp.int32) // BLOCK
    lower = row_block + offsets
    inside = (col_block[None, :] >= lower[:, None]) & (
        col_block[None, :] < (lower + widths)[:, None]
    )
    c_start = jnp.where(inside, coupling[0], jnp.zeros_like(coupling[0]))
    element = (dynamics[0], c_start, cost_matrix[0])
    results = []
    for level in range(LEVELS):
        element = level_step(element, 2**level, first)
        results.append(jnp.stack(element, axis=0)[None])
    return (results[0], results[1])


def solution(mesh):
    in_specs = (
        P("tm", "panel", None),
        P("tm", "panel", None),
        P("tm", "panel", None),
        P("tm", None),
        P("tm", None),
    )
    out_specs = (P("tm", None, "panel", None), P("tm", None, "panel", None))
    return jax.shard_map(shards, mesh=mesh, in_specs=in_specs, out_specs=out_specs, check_vma=False)
```

profile of v0, /device:TPU:1, one launch (start us, length us, event | category | flops | bytes accessed | tf_op | source)
XLA Modules:
  0.0 1131.7 jit_solution(3765280901157855510)
XLA Ops:
  7.2 0.7 all-gather.53.cloned.1.call-update
  8.0 0.8 select_reduce_fusion
  8.8 1.1 and_select_fusion
  9.9 4.9 collective-permute-start
  14.8 3.6 collective-permute-done
  18.5 54.4 %all-gather.53.cloned.1.call-done = bf16[1,1536,1536]{2,1,0:T(8,128)(2,1)} async-done(((bf16[1,96,1536]{2,1,0:T(8,128)(2,1)}), bf16[1,1536,1536]{2,1,0:T(8,128)(2,1)}) %all-gather.53.cloned.1.call-update) | async-done | bytes 4718608 | tf_op jit(solution)/shard_map/all_gather | solution.py:37
  72.9 3.9 fusion.15
  76.8 0.0 all-gather.23.cloned.1.call-start
  76.9 58.7 %all-gather.21.cloned.1.call-done = bf16[1536,1536]{1,0:T(8,128)(2,1)} async-done(((bf16[96,1536]{1,0:T(8,128)(2,1)}), bf16[1536,1536]{1,0:T(8,128)(2,1)}) %all-gather.21.cloned.1.call-update) | async-done | bytes 4718608 | tf_op jit(solution)/shard_map/all_gather | solution.py:40
  135.5 4.0 convolution_convert_fusion.12
  139.6 0.0 all-gather.25.cloned.1.call-start
  139.7 3.9 collective-permute-start.1
  143.6 3.6 collective-permute-done.1
  147.2 0.7 copy-done.12
  148.0 0.0 all-gather.27.cloned.1.call-start
  148.0 50.3 %all-gather.23.cloned.1.call-done = bf16[1536,1536]{1,0:T(8,128)(2,1)} async-done(((bf16[96,1536]{1,0:T(8,128)(2,1)}), bf16[1536,1536]{1,0:T(8,128)(2,1)}) %all-gather.23.cloned.1.call-update) | async-done | bytes 4718608 | tf_op jit(solution)/shard_map/all_gather | solution.py:43
  198.3 3.3 fusion.7
  201.6 57.6 %all-gather.25.cloned.1.call-done = bf16[1536,1536]{1,0:T(8,128)(2,1)} async-done(((bf16[96,1536]{1,0:T(8,128)(2,1)}), bf16[1536,1536]{1,0:T(8,128)(2,1)}) %all-gather.25.cloned.1.call-update) | async-done | bytes 4718608 | tf_op jit(solution)/shard_map/all_gather | solution.py:32
  259.2 3.9 convolution_convert_fusion.11
  263.1 0.0 all-gather.29.cloned.1.call-start
  263.2 0.5 all-gather.29.cloned.1.call-update
  263.8 58.1 %all-gather.27.cloned.1.call-done = bf16[1536,1536]{1,0:T(8,128)(2,1)} async-done(((bf16[96,1536]{1,0:T(8,128)(2,1)}), bf16[1536,1536]{1,0:T(8,128)(2,1)}) %all-gather.27.cloned.1.call-update) | async-done | bytes 4718608 | tf_op jit(solution)/shard_map/all_gather | solution.py:50
  321.8 3.9 fusion.27
  325.8 0.0 all-gather.55.cloned.1.call-start
  325.9 0.7 all-gather.55.cloned.1.call-update
  326.6 56.1 %all-gather.29.cloned.1.call-done = bf16[1536,1536]{1,0:T(8,128)(2,1)} async-done(((bf16[96,1536]{1,0:T(8,128)(2,1)}), bf16[1536,1536]{1,0:T(8,128)(2,1)}) %all-gather.29.cloned.1.call-update) | async-done | bytes 4718608 | tf_op jit(solution)/shard_map/all_gather | solution.py:33
  382.7 3.9 convolution_convert_fusion.10
  386.7 3.9 collective-permute-start.2
  390.6 3.6 collective-permute-done.2
  394.3 50.0 %all-gather.33.cloned.1.call-done = bf16[1536,1536]{1,0:T(8,128)(2,1)} async-done(((bf16[96,1536]{1,0:T(8,128)(2,1)}), bf16[1536,1536]{1,0:T(8,128)(2,1)}) %all-gather.33.cloned.1.call-update) | async-done | bytes 4718608 | tf_op jit(solution)/shard_map/all_gather | solution.py:63
  444.3 4.3 fusion.21
  448.7 56.6 %all-gather.55.cloned.1.call-done = bf16[1,1536,1536]{2,1,0:T(8,128)(2,1)} async-done(((bf16[1,96,1536]{2,1,0:T(8,128)(2,1)}), bf16[1,1536,1536]{2,1,0:T(8,128)(2,1)}) %all-gather.55.cloned.1.call-update) | async-done | bytes 4718608 | tf_op jit(solution)/shard_map/all_gather | solution.py:36
  505.3 61.6 %all-gather.31.cloned.1.call-done = bf16[1536,1536]{1,0:T(8,128)(2,1)} async-done(((bf16[96,1536]{1,0:T(8,128)(2,1)}), bf16[1536,1536]{1,0:T(8,128)(2,1)}) %all-gather.31.cloned.1.call-update) | async-done | bytes 4718608 | tf_op jit(solution)/shard_map/all_gather | solution.py:55
  566.9 6.1 fusion.28
  573.0 3.2 collective-permute-start.3
  576.2 5.5 collective-permute-done.3
  581.7 46.6 %all-gather.35.cloned.1.call-done = bf16[1536,1536]{1,0:T(8,128)(2,1)} async-done(((bf16[96,1536]{1,0:T(8,128)(2,1)}), bf16[1536,1536]{1,0:T(8,128)(2,1)}) %all-gather.35.cloned.1.call-update) | async-done | bytes 4718608 | tf_op jit(solution)/shard_map/all_gather | solution.py:37
  628.3 3.9 convolution_convert_fusion.9
  632.3 0.0 all-gather.39.cloned.1.call-start
  632.3 58.6 %all-gather.37.cloned.1.call-done = bf16[1536,1536]{1,0:T(8,128)(2,1)} async-done(((bf16[96,1536]{1,0:T(8,128)(2,1)}), bf16[1536,1536]{1,0:T(8,128)(2,1)}) %all-gather.37.cloned.1.call-update) | async-done | bytes 4718608 | tf_op jit(solution)/shard_map/all_gather | solution.py:40
  691.0 4.0 convolution_convert_fusion.8
  695.1 3.3 fusion.26
  698.4 3.2 collective-permute-start.4
  701.6 5.5 collective-permute-done.4
  707.1 0.7 copy-done.11
  707.9 0.5 all-gather.45.cloned.1.call-update
  708.4 45.3 %all-gather.39.cloned.1.call-done = bf16[1536,1536]{1,0:T(8,128)(2,1)} async-done(((bf16[96,1536]{1,0:T(8,128)(2,1)}), bf16[1536,1536]{1,0:T(8,128)(2,1)}) %all-gather.39.cloned.1.call-update) | async-done | bytes 4718608 | tf_op jit(solution)/shard_map/all_gather | solution.py:43
  753.8 3.2 fusion.9
  757.0 57.8 %all-gather.41.cloned.1.call-done = bf16[1536,1536]{1,0:T(8,128)(2,1)} async-done(((bf16[96,1536]{1,0:T(8,128)(2,1)}), bf16[1536,1536]{1,0:T(8,128)(2,1)}) %all-gather.41.cloned.1.call-update) | async-done | bytes 4718608 | tf_op jit(solution)/shard_map/all_gather | solution.py:32
  814.8 3.9 convolution_convert_fusion.7
  818.8 0.5 all-gather.49.cloned.1.call-update
  819.4 56.3 %all-gather.45.cloned.1.call-done = bf16[1536,1536]{1,0:T(8,128)(2,1)} async-done(((bf16[96,1536]{1,0:T(8,128)(2,1)}), bf16[1536,1536]{1,0:T(8,128)(2,1)}) %all-gather.45.cloned.1.call-update) | async-done | bytes 4718608 | tf_op jit(solution)/shard_map/all_gather | solution.py:33
  875.6 4.0 convolution_convert_fusion.5
  879.7 57.4 %all-gather.43.cloned.1.call-done = bf16[1536,1536]{1,0:T(8,128)(2,1)} async-done(((bf16[96,1536]{1,0:T(8,128)(2,1)}), bf16[1536,1536]{1,0:T(8,128)(2,1)}) %all-gather.43.cloned.1.call-update) | async-done | bytes 4718608 | tf_op jit(solution)/shard_map/all_gather | solution.py:50
  937.1 3.9 convolution_convert_fusion.3
  941.0 3.4 collective-permute-start.5
  944.4 1.0 maximum_bitcast_fusion
  945.4 52.5 %all-gather.49.cloned.1.call-done = bf16[1536,1536]{1,0:T(8,128)(2,1)} async-done(((bf16[96,1536]{1,0:T(8,128)(2,1)}), bf16[1536,1536]{1,0:T(8,128)(2,1)}) %all-gather.49.cloned.1.call-update) | async-done | bytes 4718608 | tf_op jit(solution)/shard_map/all_gather | solution.py:36
  997.9 60.9 %all-gather.47.cloned.1.call-done = bf16[1536,1536]{1,0:T(8,128)(2,1)} async-done(((bf16[96,1536]{1,0:T(8,128)(2,1)}), bf16[1536,1536]{1,0:T(8,128)(2,1)}) %all-gather.47.cloned.1.call-update) | async-done | bytes 4718608 | tf_op jit(solution)/shard_map/all_gather | solution.py:55
  1058.8 6.1 fusion.22
  1064.9 3.2 fusion.24
  1068.1 52.1 %all-gather.51.cloned.1.call-done = bf16[1536,1536]{1,0:T(8,128)(2,1)} async-done(((bf16[96,1536]{1,0:T(8,128)(2,1)}), bf16[1536,1536]{1,0:T(8,128)(2,1)}) %all-gather.51.cloned.1.call-update) | async-done | bytes 4718608 | tf_op jit(solution)/shard_map/all_gather | solution.py:63
  1120.2 3.6 fusion.23
  1123.8 1.0 maximum_bitcast_fusion.1
  (54 shorter events, 0.8 us)
Async XLA Ops:
  7.2 65.7 %all-gather.53.cloned.1.call-start = ((), (), s32[]{:S(2)}) async-start(), calls=%async_computation.16 | async-start | bytes 5013504 | tf_op jit(solution)/shard_map/all_gather | solution.py:37
  7.9 127.6 %all-gather.21.cloned.1.call-start = ((), (), s32[]{:S(2)}) async-start(), calls=%async_computation | async-start | bytes 5013504 | tf_op jit(solution)/shard_map/all_gather | solution.py:40
  9.9 8.6 collective-permute-start
  18.5 121.1 %copy-start.9 = (bf16[96,1536]{1,0:T(8,128)(2,1)}, bf16[96,1536]{1,0:T(8,128)(2,1)S(1)}, u32[]{:S(2)}) copy-start(bf16[96,1536]{1,0:T(8,128)(2,1)S(1)} %collective-permute-done) | copy-start | bytes 884740
  18.5 121.2 %copy-start.7 = (bf16[1,96,1536]{2,1,0:T(8,128)(2,1)S(1)}, bf16[1,96,1536]{2,1,0:T(8,128)(2,1)}, u32[]{:S(2)}) copy-start(bf16[1,96,1536]{2,1,0:T(8,128)(2,1)} %param.5) | copy-start | bytes 884740
  76.8 121.5 %copy-start.4 = (bf16[96,1536]{1,0:T(8,128)(2,1)S(1)}, bf16[96,1536]{1,0:T(8,128)(2,1)}, u32[]{:S(2)}) copy-start(bf16[96,1536]{1,0:T(8,128)(2,1)} %fusion.15) | copy-start | bytes 884740
  76.8 121.5 %all-gather.23.cloned.1.call-start = ((), (), s32[]{:S(2)}) async-start(), calls=%async_computation.1 | async-start | bytes 5013504 | tf_op jit(solution)/shard_map/all_gather | solution.py:43
  139.6 119.6 %all-gather.25.cloned.1.call-start = ((), (), s32[]{:S(2)}) async-start(), calls=%async_computation.2 | async-start | bytes 5013504 | tf_op jit(solution)/shard_map/all_gather | solution.py:32
  139.7 7.6 collective-permute-start.1
  147.2 0.7 copy-start.12
  148.0 173.9 %all-gather.27.cloned.1.call-start = ((), (), s32[]{:S(2)}) async-start(), calls=%async_computation.3 | async-start | bytes 5013504 | tf_op jit(solution)/shard_map/all_gather | solution.py:50
  148.0 173.8 %copy-start.5 = (bf16[1,96,1536]{2,1,0:T(8,128)(2,1)S(1)}, bf16[1,96,1536]{2,1,0:T(8,128)(2,1)}, u32[]{:S(2)}) copy-start(bf16[1,96,1536]{2,1,0:T(8,128)(2,1)} %param.7) | copy-start | bytes 884740
  263.1 119.6 %all-gather.29.cloned.1.call-start = ((), (), s32[]{:S(2)}) async-start(), calls=%async_computation.4 | async-start | bytes 5013504 | tf_op jit(solution)/shard_map/all_gather | solution.py:33
  263.7 180.6 %all-gather.33.cloned.1.call-start = ((), (), s32[]{:S(2)}) async-start(), calls=%async_computation.6 | async-start | bytes 5013504 | tf_op jit(solution)/shard_map/all_gather | solution.py:63
  325.8 179.5 %all-gather.55.cloned.1.call-start = ((), (), s32[]{:S(2)}) async-start(), calls=%async_computation.17 | async-start | bytes 5013504 | tf_op jit(solution)/shard_map/all_gather | solution.py:36
  326.6 240.3 %copy-start.8 = (bf16[1,96,1536]{2,1,0:T(8,128)(2,1)S(1)}, bf16[1,96,1536]{2,1,0:T(8,128)(2,1)}, u32[]{:S(2)}) copy-start(bf16[1,96,1536]{2,1,0:T(8,128)(2,1)} %param.5) | copy-start | bytes 884740
  326.6 240.3 %all-gather.31.cloned.1.call-start = ((), (), s32[]{:S(2)}) async-start(), calls=%async_computation.5 | async-start | bytes 5013504 | tf_op jit(solution)/shard_map/all_gather | solution.py:55
  386.7 241.7 %all-gather.35.cloned.1.call-start = ((), (), s32[]{:S(2)}) async-start(), calls=%async_computation.7 | async-start | bytes 5013504 | tf_op jit(solution)/shard_map/all_gather | solution.py:37
  386.7 7.6 collective-permute-start.2
  448.6 242.4 %all-gather.37.cloned.1.call-start = ((), (), s32[]{:S(2)}) async-start(), calls=%async_computation.8 | async-start | bytes 5013504 | tf_op jit(solution)/shard_map/all_gather | solution.py:40
  573.0 8.7 collective-permute-start.3
  581.7 113.3 %copy-start.10 = (bf16[96,1536]{1,0:T(8,128)(2,1)}, bf16[96,1536]{1,0:T(8,128)(2,1)S(1)}, u32[]{:S(2)}) copy-start(bf16[96,1536]{1,0:T(8,128)(2,1)S(1)} %collective-permute-done.3) | copy-start | bytes 884740
  632.3 121.5 %copy-start.3 = (bf16[96,1536]{1,0:T(8,128)(2,1)S(1)}, bf16[96,1536]{1,0:T(8,128)(2,1)}, u32[]{:S(2)}) copy-start(bf16[96,1536]{1,0:T(8,128)(2,1)} %convolution_convert_fusion.9) | copy-start | bytes 884740
  632.3 121.5 %all-gather.39.cloned.1.call-start = ((), (), s32[]{:S(2)}) async-start(), calls=%async_computation.9 | async-start | bytes 5013504 | tf_op jit(solution)/shard_map/all_gather | solution.py:43
  695.0 58.7 %copy-start.6 = (bf16[96,1536]{1,0:T(8,128)(2,1)S(1)}, bf16[96,1536]{1,0:T(8,128)(2,1)}, u32[]{:S(2)}) copy-start(bf16[96,1536]{1,0:T(8,128)(2,1)} %convolution_convert_fusion.8) | copy-start | bytes 884740
  695.1 119.7 %all-gather.41.cloned.1.call-start = ((), (), s32[]{:S(2)}) async-start(), calls=%async_computation.10 | async-start | bytes 5013504 | tf_op jit(solution)/shard_map/all_gather | solution.py:32
  698.4 120.3 %copy-start.1 = (bf16[96,1536]{1,0:T(8,128)(2,1)}, bf16[96,1536]{1,0:T(8,128)(2,1)S(1)}, u32[]{:S(2)}) copy-start(bf16[96,1536]{1,0:T(8,128)(2,1)S(1)} %fusion.26) | copy-start | bytes 884740
  698.4 8.7 collective-permute-start.4
  707.1 0.7 copy-start.11
  707.8 167.8 %all-gather.45.cloned.1.call-start = ((), (), s32[]{:S(2)}) async-start(), calls=%async_computation.12 | async-start | bytes 5013504 | tf_op jit(solution)/shard_map/all_gather | solution.py:33
  708.4 228.7 %all-gather.43.cloned.1.call-start = ((), (), s32[]{:S(2)}) async-start(), calls=%async_computation.11 | async-start | bytes 5013504 | tf_op jit(solution)/shard_map/all_gather | solution.py:50
  757.0 180.1 %copy-start = (bf16[96,1536]{1,0:T(8,128)(2,1)S(1)}, bf16[96,1536]{1,0:T(8,128)(2,1)}, u32[]{:S(2)}) copy-start(bf16[96,1536]{1,0:T(8,128)(2,1)} %fusion.21) | copy-start | bytes 884740
  818.7 179.2 %all-gather.49.cloned.1.call-start = ((), (), s32[]{:S(2)}) async-start(), calls=%async_computation.14 | async-start | bytes 5013504 | tf_op jit(solution)/shard_map/all_gather | solution.py:36
  819.3 125.1 %copy-start.2 = (bf16[96,1536]{1,0:T(8,128)(2,1)S(1)}, bf16[96,1536]{1,0:T(8,128)(2,1)}, u32[]{:S(2)}) copy-start(bf16[96,1536]{1,0:T(8,128)(2,1)} %copy-done.1) | copy-start | bytes 884740
  819.3 239.5 %all-gather.47.cloned.1.call-start = ((), (), s32[]{:S(2)}) async-start(), calls=%async_computation.13 | async-start | bytes 5013504 | tf_op jit(solution)/shard_map/all_gather | solution.py:55
  879.6 240.6 %all-gather.51.cloned.1.call-start = ((), (), s32[]{:S(2)}) async-start(), calls=%async_computation.15 | async-start | bytes 5013504 | tf_op jit(solution)/shard_map/all_gather | solution.py:63
  941.0 127.1 %collective-permute-start.5 = (bf16[96,1536]{1,0:T(8,128)(2,1)S(1)}, bf16[96,1536]{1,0:T(8,128)(2,1)S(1)}, u32[]{:S(2)}, u32[]{:S(2)}) collective-permute-start(bf16[96,1536]{1,0:T(8,128)(2,1)S(1)} %copy-done), channel_id=1, source_target_pairs={{0,32},{16,48},{32,64},{48,80},{64,96},{80,112},{96,128},{112,144}... | collective-permute-start | bytes 884744 | tf_op jit(solution)/shard_map/ppermute | solution.py:13
Sparse Core Ops, SparseCore 0:
  10.4 62.4 all-gather.52
  76.9 58.5 all-gather.20
  139.7 58.5 all-gather.22
  200.6 58.5 all-gather.24
  263.3 58.5 all-gather.26
  324.1 58.5 all-gather.28
  385.7 58.5 all-gather.32
  446.7 58.5 all-gather.54
  508.3 58.5 all-gather.30
  569.7 58.5 all-gather.34
  632.4 58.5 all-gather.36
  695.2 58.5 all-gather.38
  756.2 58.5 all-gather.40
  817.1 58.5 all-gather.44
  878.5 58.5 all-gather.42
  939.4 58.5 all-gather.48
  1000.2 58.5 all-gather.46
  1061.7 58.5 all-gather.50
where the time goes:
time: 1130 us
  waiting for transfers between devices  1020 us (90%)
  matrix products  72.6 us (6%)
  starting transfers between devices  23.2 us (2%)
  between operations  14.5 us (1%)
    all_gather x2, waiting for transfers between devices, level_step(): lax.all_gather(v_rows, 'panel', axis=0, tiled=True)  122 us
    all_gather x2, waiting for transfers between devices, level_step(): lax.all_gather(k_rows, 'panel', axis=0, tiled=True)  117 us
    all_gather x2, waiting for transfers between devices, level_step(): lax.all_gather(u_rows, 'panel', axis=0, tiled=True)  115 us
    all_gather x2, waiting for transfers between devices, level_step(): lax.all_gather(a_part, 'panel', axis=0, tiled=True)  115 us
    all_gather x2, waiting for transfers between devices, level_step(): lax.all_gather(c_part, 'panel', axis=0, tiled=True)  112 us
    all_gather x2, waiting for transfers between devices, level_step(): lax.all_gather(a_own, 'panel', axis=0, tiled=True)  109 us
    all_gather x2, waiting for transfers between devices, level_step(): lax.all_gather(s_rows, 'panel', axis=0, tiled=True)  102 us
    all_gather x2, waiting for transfers between devices, level_step(): lax.all_gather(j_own, 'panel', axis=0, tiled=True)  101 us
  transfers between devices with their start and end apart: 24, of which 23 were waited for; matrix products, arithmetic and copies ran while one was open for 5% of the time, Pallas kernels for 0%

commit v1 on v0

--- a/solution.py
+++ b/solution.py
@@ -5,6 +5,19 @@
 
 BLOCK = 128
 LEVELS = 2
+
+
+def ring_gather(shard, axis, dim):
+    ways = lax.axis_size(axis)
+    up = [(d, (d + 1) % ways) for d in range(ways)]
+    down = [(d, (d - 1) % ways) for d in range(ways)]
+    earlier, later = ([shard], [shard])
+    for _ in range(ways // 2):
+        earlier.append(lax.ppermute(earlier[-1], axis, up))
+    for _ in range((ways - 1) // 2):
+        later.append(lax.ppermute(later[-1], axis, down))
+    line = jnp.concatenate([*earlier[::-1], *later[1:]], axis=dim)
+    return jnp.roll(line, (lax.axis_index(axis) - ways // 2) * shard.shape[dim], axis=dim)
 
 
 def passed_along(value, axis, by):
@@ -37,9 +50,7 @@
         lax.all_gather(j_own, "panel", axis=0, tiled=True),
     )
     k_rows = jnp.dot(c_part, j_full, preferred_element_type=jnp.float32).astype(jnp.bfloat16)
-    q_rows = contract_rows(k_rows, lax.all_gather(k_rows, "panel", axis=0, tiled=True)).astype(
-        jnp.bfloat16
-    )
+    q_rows = contract_rows(k_rows, ring_gather(k_rows, "panel", 0)).astype(jnp.bfloat16)
     k_q = contract_rows(k_rows, lax.all_gather(q_rows, "panel", axis=0, tiled=True))
     row_ids = first + jnp.arange(rows, dtype=jnp.int32)
     identity = (row_ids[:, None] == jnp.arange(width, dtype=jnp.int32)[None, :]).astype(jnp.float32)

time: 1130 us -> 1200 us (1.062)
  starting transfers between devices: 23.2 us -> 102 us
  waiting for transfers between devices: 1020 us -> 990 us
    all_gather x2 -> x0, waiting for transfers between devices: 117 us -> none  [level_step(): lax.all_gather(k_rows, 'panel', axis=0, tiled=True)]
    ppermute x0 -> x30, waiting for transfers between devices: none -> 83.6 us  [the longest x16 83.6 us: ring_gather(): earlier.append(lax.ppermute(earlier[-1], axis, up))]
    ppermute x0 -> x30, starting transfers between devices: none -> 70.9 us  [the longest x14 68.1 us: ring_gather(): later.append(lax.ppermute(later[-1], axis, down))]
  transfers between devices with their start and end apart: 24 -> 52, of which waited for: 23 -> 37; matrix products, arithmetic and copies ran while one was open for 5% -> 5% of each run, Pallas kernels for 0% -> 0%
where the time goes in v1:
time: 1200 us; the launch traced here: 1190 us
  waiting for transfers between devices  990 us (82%)
  starting transfers between devices  102 us (8%)
  matrix products  72.6 us (6%)
  between operations  14.7 us (1%)
    all_gather x2, waiting for transfers between devices, level_step(): lax.all_gather(v_rows, 'panel', axis=0, tiled=True)  122 us
    all_gather x2, waiting for transfers between devices, level_step(): lax.all_gather(a_part, 'panel', axis=0, tiled=True)  116 us
    all_gather x2, waiting for transfers between devices, level_step(): lax.all_gather(u_rows, 'panel', axis=0, tiled=True)  116 us
    all_gather x2, waiting for transfers between devices, level_step(): lax.all_gather(c_part, 'panel', axis=0, tiled=True)  112 us
    all_gather x2, waiting for transfers between devices, level_step(): lax.all_gather(a_own, 'panel', axis=0, tiled=True)  109 us
    all_gather x2, waiting for transfers between devices, level_step(): lax.all_gather(q_rows, 'panel', axis=0, tiled=True)  104 us
    all_gather x2, waiting for transfers between devices, level_step(): lax.all_gather(s_rows, 'panel', axis=0, tiled=True)  102 us
    all_gather x2, waiting for transfers between devices, level_step(): lax.all_gather(j_own, 'panel', axis=0, tiled=True)  101 us
  transfers between devices with their start and end apart: 52, of which 37 were waited for; matrix products, arithmetic and copies ran while one was open for 5% of the time, Pallas kernels for 0%

profile of v1, /device:TPU:1, one launch (start us, length us, event | category | flops | bytes accessed | tf_op | source)
XLA Modules:
  0.0 1190.2 jit_solution(13725953595227496020)
XLA Ops:
  9.9 4.9 collective-permute-start
  14.8 3.6 collective-permute-done
  18.5 54.4 %all-gather.47.cloned.1.call-done = bf16[1,1536,1536]{2,1,0:T(8,128)(2,1)} async-done(((bf16[1,96,1536]{2,1,0:T(8,128)(2,1)}), bf16[1,1536,1536]{2,1,0:T(8,128)(2,1)}) %all-gather.47.cloned.1.call-update) | async-done | bytes 4718608 | tf_op jit(solution)/shard_map/all_gather | solution.py:50
  77.4 9.9 collective-permute-done.1
  87.2 4.8 collective-permute-start.9
  92.0 5.4 collective-permute-done.2
  97.4 4.8 collective-permute-start.10
  102.2 4.5 collective-permute-done.3
  106.7 4.8 collective-permute-start.11
  111.5 4.1 collective-permute-done.4
  115.6 4.8 collective-permute-start.12
  120.4 4.1 collective-permute-done.5
  124.5 4.8 collective-permute-start.13
  129.3 4.1 collective-permute-done.6
  133.4 4.8 collective-permute-start.14
  138.2 4.6 collective-permute-done.7
  142.9 5.5 collective-permute-start.15
  148.4 5.0 collective-permute-done.8
  158.6 4.8 fusion.22
  163.5 12.2 %collective-permute-start.16 = (bf16[96,1536]{1,0:T(8,128)(2,1)S(1)}, bf16[96,1536]{1,0:T(8,128)(2,1)S(1)}, u32[]{:S(2)}, u32[]{:S(2)}) collective-permute-start(bf16[96,1536]{1,0:T(8,128)(2,1)S(1)} %bitcast.79), channel_id=1, source_target_pairs={{0,16},{16,32},{32,48},{48,64},{64,80},{80,96},{96,112},{112,128},... | collective-permute-start | bytes 884744 | tf_op jit(solution)/shard_map/ppermute | solution.py:26
  175.7 3.6 collective-permute-done.16
  180.2 47.0 %all-gather.19.cloned.1.call-done = bf16[1536,1536]{1,0:T(8,128)(2,1)} async-done(((bf16[96,1536]{1,0:T(8,128)(2,1)}), bf16[1536,1536]{1,0:T(8,128)(2,1)}) %all-gather.19.cloned.1.call-update) | async-done | bytes 4718608 | tf_op jit(solution)/shard_map/all_gather | solution.py:54
  230.4 58.3 %all-gather.21.cloned.1.call-done = bf16[1536,1536]{1,0:T(8,128)(2,1)} async-done(((bf16[96,1536]{1,0:T(8,128)(2,1)}), bf16[1536,1536]{1,0:T(8,128)(2,1)}) %all-gather.21.cloned.1.call-update) | async-done | bytes 4718608 | tf_op jit(solution)/shard_map/all_gather | solution.py:45
  288.7 3.9 convolution_convert_fusion.10
  293.3 58.1 %all-gather.23.cloned.1.call-done = bf16[1536,1536]{1,0:T(8,128)(2,1)} async-done(((bf16[96,1536]{1,0:T(8,128)(2,1)}), bf16[1536,1536]{1,0:T(8,128)(2,1)}) %all-gather.23.cloned.1.call-update) | async-done | bytes 4718608 | tf_op jit(solution)/shard_map/all_gather | solution.py:61
  351.4 3.9 fusion.37
  356.2 56.1 %all-gather.25.cloned.1.call-done = bf16[1536,1536]{1,0:T(8,128)(2,1)} async-done(((bf16[96,1536]{1,0:T(8,128)(2,1)}), bf16[1536,1536]{1,0:T(8,128)(2,1)}) %all-gather.25.cloned.1.call-update) | async-done | bytes 4718608 | tf_op jit(solution)/shard_map/all_gather | solution.py:46
  412.2 3.9 convolution_convert_fusion.9
  416.2 3.9 collective-permute-start.17
  420.2 3.6 collective-permute-done.17
  423.8 49.9 %all-gather.29.cloned.1.call-done = bf16[1536,1536]{1,0:T(8,128)(2,1)} async-done(((bf16[96,1536]{1,0:T(8,128)(2,1)}), bf16[1536,1536]{1,0:T(8,128)(2,1)}) %all-gather.29.cloned.1.call-update) | async-done | bytes 4718608 | tf_op jit(solution)/shard_map/all_gather | solution.py:74
  473.7 4.3 fusion.31
  478.1 56.6 %all-gather.49.cloned.1.call-done = bf16[1,1536,1536]{2,1,0:T(8,128)(2,1)} async-done(((bf16[1,96,1536]{2,1,0:T(8,128)(2,1)}), bf16[1,1536,1536]{2,1,0:T(8,128)(2,1)}) %all-gather.49.cloned.1.call-update) | async-done | bytes 4718608 | tf_op jit(solution)/shard_map/all_gather | solution.py:49
  534.7 61.6 %all-gather.27.cloned.1.call-done = bf16[1536,1536]{1,0:T(8,128)(2,1)} async-done(((bf16[96,1536]{1,0:T(8,128)(2,1)}), bf16[1536,1536]{1,0:T(8,128)(2,1)}) %all-gather.27.cloned.1.call-update) | async-done | bytes 4718608 | tf_op jit(solution)/shard_map/all_gather | solution.py:66
  596.3 6.1 fusion.38
  605.6 5.5 collective-permute-done.18
  611.0 46.8 %all-gather.31.cloned.1.call-done = bf16[1536,1536]{1,0:T(8,128)(2,1)} async-done(((bf16[96,1536]{1,0:T(8,128)(2,1)}), bf16[1536,1536]{1,0:T(8,128)(2,1)}) %all-gather.31.cloned.1.call-update) | async-done | bytes 4718608 | tf_op jit(solution)/shard_map/all_gather | solution.py:50
  662.3 9.9 collective-permute-done.19
  672.4 4.8 collective-permute-start.27
  677.1 5.4 collective-permute-done.20
  682.5 4.8 collective-permute-start.28
  687.3 4.5 collective-permute-done.21
  691.9 4.8 collective-permute-start.29
  696.7 4.1 collective-permute-done.22
  700.8 4.8 collective-permute-start.30
  705.6 4.1 collective-permute-done.23
  709.7 4.8 collective-permute-start.31
  714.4 4.1 collective-permute-done.24
  718.6 4.8 collective-permute-start.32
  723.3 4.5 collective-permute-done.25
  727.9 5.3 collective-permute-start.33
  733.1 5.2 collective-permute-done.26
  738.8 4.8 fusion.19
  755.2 57.1 %all-gather.33.cloned.1.call-done = bf16[1536,1536]{1,0:T(8,128)(2,1)} async-done(((bf16[96,1536]{1,0:T(8,128)(2,1)}), bf16[1536,1536]{1,0:T(8,128)(2,1)}) %all-gather.33.cloned.1.call-update) | async-done | bytes 4718608 | tf_op jit(solution)/shard_map/all_gather | solution.py:54
  815.5 57.8 %all-gather.35.cloned.1.call-done = bf16[1536,1536]{1,0:T(8,128)(2,1)} async-done(((bf16[96,1536]{1,0:T(8,128)(2,1)}), bf16[1536,1536]{1,0:T(8,128)(2,1)}) %all-gather.35.cloned.1.call-update) | async-done | bytes 4718608 | tf_op jit(solution)/shard_map/all_gather | solution.py:45
  873.3 3.9 convolution_convert_fusion.7
  877.9 56.3 %all-gather.39.cloned.1.call-done = bf16[1536,1536]{1,0:T(8,128)(2,1)} async-done(((bf16[96,1536]{1,0:T(8,128)(2,1)}), bf16[1536,1536]{1,0:T(8,128)(2,1)}) %all-gather.39.cloned.1.call-update) | async-done | bytes 4718608 | tf_op jit(solution)/shard_map/all_gather | solution.py:46
  934.1 3.9 convolution_convert_fusion.5
  938.1 57.6 %all-gather.37.cloned.1.call-done = bf16[1536,1536]{1,0:T(8,128)(2,1)} async-done(((bf16[96,1536]{1,0:T(8,128)(2,1)}), bf16[1536,1536]{1,0:T(8,128)(2,1)}) %all-gather.37.cloned.1.call-update) | async-done | bytes 4718608 | tf_op jit(solution)/shard_map/all_gather | solution.py:61
  995.7 3.9 convolution_convert_fusion.3
  1003.9 52.7 %all-gather.43.cloned.1.call-done = bf16[1536,1536]{1,0:T(8,128)(2,1)} async-done(((bf16[96,1536]{1,0:T(8,128)(2,1)}), bf16[1536,1536]{1,0:T(8,128)(2,1)}) %all-gather.43.cloned.1.call-update) | async-done | bytes 4718608 | tf_op jit(solution)/shard_map/all_gather | solution.py:49
  1056.6 60.9 %all-gather.41.cloned.1.call-done = bf16[1536,1536]{1,0:T(8,128)(2,1)} async-done(((bf16[96,1536]{1,0:T(8,128)(2,1)}), bf16[1536,1536]{1,0:T(8,128)(2,1)}) %all-gather.41.cloned.1.call-update) | async-done | bytes 4718608 | tf_op jit(solution)/shard_map/all_gather | solution.py:66
  1117.4 6.1 fusion.32
  1126.7 52.1 %all-gather.45.cloned.1.call-done = bf16[1536,1536]{1,0:T(8,128)(2,1)} async-done(((bf16[96,1536]{1,0:T(8,128)(2,1)}), bf16[1536,1536]{1,0:T(8,128)(2,1)}) %all-gather.45.cloned.1.call-update) | async-done | bytes 4718608 | tf_op jit(solution)/shard_map/all_gather | solution.py:74
  (140 shorter events, 53.7 us)
Async XLA Ops:
  7.2 65.7 %all-gather.47.cloned.1.call-start = ((), (), s32[]{:S(2)}) async-start(), calls=%async_computation.14 | async-start | bytes 5013504 | tf_op jit(solution)/shard_map/all_gather | solution.py:50
  7.9 219.2 %all-gather.19.cloned.1.call-start = ((), (), s32[]{:S(2)}) async-start(), calls=%async_computation | async-start | bytes 5013504 | tf_op jit(solution)/shard_map/all_gather | solution.py:54
  9.9 8.6 collective-permute-start
  18.5 138.9 %copy-start.7 = (bf16[96,1536]{1,0:T(8,128)(2,1)}, bf16[96,1536]{1,0:T(8,128)(2,1)S(1)}, u32[]{:S(2)}) copy-start(bf16[96,1536]{1,0:T(8,128)(2,1)S(1)} %collective-permute-done) | copy-start | bytes 884740
  76.1 11.1 collective-permute-start.1
  87.2 10.2 collective-permute-start.2
  87.2 10.2 collective-permute-start.9
  97.4 9.3 collective-permute-start.3
  97.4 9.3 collective-permute-start.10
  106.7 8.9 collective-permute-start.4
  106.7 8.9 collective-permute-start.11
  115.6 8.9 collective-permute-start.5
  115.6 8.9 collective-permute-start.12
  124.5 8.9 copy-start.9
  124.5 8.9 collective-permute-start.6
  124.5 8.9 collective-permute-start.13
  133.4 4.8 copy-start.10
  133.4 9.4 collective-permute-start.7
  133.4 9.4 collective-permute-start.14
  142.8 10.5 collective-permute-start.8
  142.9 15.7 %collective-permute-start.15 = (bf16[96,1536]{1,0:T(8,128)(2,1)}, bf16[96,1536]{1,0:T(8,128)(2,1)S(1)}, u32[]{:S(2)}, u32[]{:S(2)}) collective-permute-start(bf16[96,1536]{1,0:T(8,128)(2,1)} %collective-permute-done.14), channel_id=1, source_target_pairs={{0,15},{1,0},{2,1},{3,2},{4,3},{5,4},{6,5},{7,6},{8,7},{9,8},{10,9... | collective-permute-start | bytes 884744 | tf_op jit(solution)/shard_map/ppermute | solution.py:18
  158.6 4.9 copy-start.4
  163.4 125.3 %all-gather.21.cloned.1.call-start = ((), (), s32[]{:S(2)}) async-start(), calls=%async_computation.1 | async-start | bytes 5013504 | tf_op jit(solution)/shard_map/all_gather | solution.py:45
  163.5 15.9 %collective-permute-start.16 = (bf16[96,1536]{1,0:T(8,128)(2,1)S(1)}, bf16[96,1536]{1,0:T(8,128)(2,1)S(1)}, u32[]{:S(2)}, u32[]{:S(2)}) collective-permute-start(bf16[96,1536]{1,0:T(8,128)(2,1)S(1)} %bitcast.79), channel_id=1, source_target_pairs={{0,16},{16,32},{32,48},{48,64},{64,80},{80,96},{96,112},{112,128},... | collective-permute-start | bytes 884744 | tf_op jit(solution)/shard_map/ppermute | solution.py:26
  179.3 0.7 copy-start.12
  180.1 171.3 %all-gather.23.cloned.1.call-start = ((), (), s32[]{:S(2)}) async-start(), calls=%async_computation.2 | async-start | bytes 5013504 | tf_op jit(solution)/shard_map/all_gather | solution.py:61
  180.1 171.2 %copy-start.3 = (bf16[1,96,1536]{2,1,0:T(8,128)(2,1)S(1)}, bf16[1,96,1536]{2,1,0:T(8,128)(2,1)}, u32[]{:S(2)}) copy-start(bf16[1,96,1536]{2,1,0:T(8,128)(2,1)} %param.9) | copy-start | bytes 884740
  292.7 119.6 %all-gather.25.cloned.1.call-start = ((), (), s32[]{:S(2)}) async-start(), calls=%async_computation.3 | async-start | bytes 5013504 | tf_op jit(solution)/shard_map/all_gather | solution.py:46
  293.3 180.4 %all-gather.29.cloned.1.call-start = ((), (), s32[]{:S(2)}) async-start(), calls=%async_computation.5 | async-start | bytes 5013504 | tf_op jit(solution)/shard_map/all_gather | solution.py:74
  355.3 179.3 %all-gather.49.cloned.1.call-start = ((), (), s32[]{:S(2)}) async-start(), calls=%async_computation.15 | async-start | bytes 5013504 | tf_op jit(solution)/shard_map/all_gather | solution.py:49
  356.1 240.2 %copy-start.5 = (bf16[1,96,1536]{2,1,0:T(8,128)(2,1)S(1)}, bf16[1,96,1536]{2,1,0:T(8,128)(2,1)}, u32[]{:S(2)}) copy-start(bf16[1,96,1536]{2,1,0:T(8,128)(2,1)} %param.7) | copy-start | bytes 884740
  356.1 240.2 %all-gather.27.cloned.1.call-start = ((), (), s32[]{:S(2)}) async-start(), calls=%async_computation.4 | async-start | bytes 5013504 | tf_op jit(solution)/shard_map/all_gather | solution.py:66
  416.2 241.7 %all-gather.31.cloned.1.call-start = ((), (), s32[]{:S(2)}) async-start(), calls=%async_computation.6 | async-start | bytes 5013504 | tf_op jit(solution)/shard_map/all_gather | solution.py:50
  416.2 7.6 collective-permute-start.17
  478.0 334.2 %all-gather.33.cloned.1.call-start = ((), (), s32[]{:S(2)}) async-start(), calls=%async_computation.7 | async-start | bytes 5013504 | tf_op jit(solution)/shard_map/all_gather | solution.py:54
  602.4 8.7 collective-permute-start.18
  611.0 127.5 %copy-start.8 = (bf16[96,1536]{1,0:T(8,128)(2,1)}, bf16[96,1536]{1,0:T(8,128)(2,1)S(1)}, u32[]{:S(2)}) copy-start(bf16[96,1536]{1,0:T(8,128)(2,1)S(1)} %collective-permute-done.18) | copy-start | bytes 884740
  661.1 11.1 collective-permute-start.19
  672.2 10.3 collective-permute-start.20
  672.4 10.2 collective-permute-start.27
  682.5 9.3 collective-permute-start.21
  682.5 9.3 collective-permute-start.28
  691.9 8.9 collective-permute-start.22
  691.9 8.9 collective-permute-start.29
  700.8 8.9 collective-permute-start.23
  700.8 8.9 collective-permute-start.30
  709.7 8.9 collective-permute-start.24
  709.7 8.9 collective-permute-start.31
  718.6 9.3 collective-permute-start.25
  718.6 9.3 collective-permute-start.32
  727.9 10.5 collective-permute-start.26
  727.9 10.9 collective-permute-start.33
  743.6 68.6 %copy-start.6 = (bf16[96,1536]{1,0:T(8,128)(2,1)S(1)}, bf16[96,1536]{1,0:T(8,128)(2,1)}, u32[]{:S(2)}) copy-start(bf16[96,1536]{1,0:T(8,128)(2,1)} %fusion.19) | copy-start | bytes 884740
  743.6 129.6 %all-gather.35.cloned.1.call-start = ((), (), s32[]{:S(2)}) async-start(), calls=%async_computation.8 | async-start | bytes 5013504 | tf_op jit(solution)/shard_map/all_gather | solution.py:45
  746.9 130.2 %copy-start.1 = (bf16[96,1536]{1,0:T(8,128)(2,1)}, bf16[96,1536]{1,0:T(8,128)(2,1)S(1)}, u32[]{:S(2)}) copy-start(bf16[96,1536]{1,0:T(8,128)(2,1)S(1)} %fusion.36) | copy-start | bytes 884740
  747.0 6.8 collective-permute-start.34
  754.5 179.6 %all-gather.39.cloned.1.call-start = ((), (), s32[]{:S(2)}) async-start(), calls=%async_computation.10 | async-start | bytes 5013504 | tf_op jit(solution)/shard_map/all_gather | solution.py:46
  755.1 240.6 %all-gather.37.cloned.1.call-start = ((), (), s32[]{:S(2)}) async-start(), calls=%async_computation.9 | async-start | bytes 5013504 | tf_op jit(solution)/shard_map/all_gather | solution.py:61
  815.5 180.2 %copy-start = (bf16[96,1536]{1,0:T(8,128)(2,1)S(1)}, bf16[96,1536]{1,0:T(8,128)(2,1)}, u32[]{:S(2)}) copy-start(bf16[96,1536]{1,0:T(8,128)(2,1)} %fusion.31) | copy-start | bytes 884740
  877.2 179.4 %all-gather.43.cloned.1.call-start = ((), (), s32[]{:S(2)}) async-start(), calls=%async_computation.12 | async-start | bytes 5013504 | tf_op jit(solution)/shard_map/all_gather | solution.py:49
  877.8 125.1 %copy-start.2 = (bf16[96,1536]{1,0:T(8,128)(2,1)S(1)}, bf16[96,1536]{1,0:T(8,128)(2,1)}, u32[]{:S(2)}) copy-start(bf16[96,1536]{1,0:T(8,128)(2,1)} %copy-done.1) | copy-start | bytes 884740
  877.8 239.6 %all-gather.41.cloned.1.call-start = ((), (), s32[]{:S(2)}) async-start(), calls=%async_computation.11 | async-start | bytes 5013504 | tf_op jit(solution)/shard_map/all_gather | solution.py:66
  938.1 240.8 %all-gather.45.cloned.1.call-start = ((), (), s32[]{:S(2)}) async-start(), calls=%async_computation.13 | async-start | bytes 5013504 | tf_op jit(solution)/shard_map/all_gather | solution.py:74
  999.7 127.1 %collective-permute-start.35 = (bf16[96,1536]{1,0:T(8,128)(2,1)S(1)}, bf16[96,1536]{1,0:T(8,128)(2,1)S(1)}, u32[]{:S(2)}, u32[]{:S(2)}) collective-permute-start(bf16[96,1536]{1,0:T(8,128)(2,1)S(1)} %copy-done), channel_id=1, source_target_pairs={{0,32},{16,48},{32,64},{48,80},{64,96},{80,112},{96,128},{112,144}... | collective-permute-start | bytes 884744 | tf_op jit(solution)/shard_map/ppermute | solution.py:26
  (1 other events, 0.7 us)
Sparse Core Ops, SparseCore 0:
  10.4 62.4 all-gather.46
  163.5 63.5 all-gather.18
  230.1 58.5 all-gather.20
  292.8 58.5 all-gather.22
  353.6 58.5 all-gather.24
  415.1 58.5 all-gather.28
  476.1 58.5 all-gather.48
  537.7 58.5 all-gather.26
  599.3 58.5 all-gather.30
  743.8 68.4 all-gather.32
  814.7 58.5 all-gather.34
  875.5 58.5 all-gather.38
  937.1 58.5 all-gather.36
  998.0 58.5 all-gather.42
  1058.8 58.5 all-gather.40
  1120.3 58.5 all-gather.44
